TPU v7x, 512 devices: a whole 4x4x16 slice. The times are simulated.
512 devices in a mesh: dp: 16 (over x, y), mp: 32 (over z, core).
Axes of the slice: x: 4, y: 4, z: 16, core: 2. Of those that a mesh axis runs over, the one named last changes fastest.
Arguments:
- hidden_policy: bfloat16 [256, 16, 2048], P('dp', None, 'mp'), may hold values from -6 to 6
- hidden_reference: bfloat16 [256, 16, 2048], P('dp', None, 'mp'), may hold values from -6 to 6
- ffn_gain_policy: float32 [2048], replicated, may hold values from 0.1 to 1.9
- ffn_gain_reference: float32 [2048], replicated, may hold values from 0.1 to 1.9
- up_policy: bfloat16 [2048, 4096], P(None, 'mp'), may hold values from -0.125 to 0.125
- up_reference: bfloat16 [2048, 4096], P(None, 'mp'), may hold values from -0.125 to 0.125
- down_policy: bfloat16 [4096, 2048], P('mp'), may hold values from -0.1875 to 0.1875
- down_reference: bfloat16 [4096, 2048], P('mp'), may hold values from -0.1875 to 0.1875
- final_gain_policy: float32 [2048], replicated, may hold values from 0.1 to 1.9
- final_gain_reference: float32 [2048], replicated, may hold values from 0.1 to 1.9
- out_policy: bfloat16 [2048, 28672], P('dp', 'mp'), may hold values from -4 to 4
- out_reference: bfloat16 [2048, 28672], P('dp', 'mp'), may hold values from -4 to 4
- move_plan: int32 [256], replicated, may hold values from 0 to 255, as said below
- lengths: int32 [256], P('dp'), may hold values from 1 to 16, 2048 in all
- targets: int32 [256, 16], P('dp'), may hold values from 0 to 28671
Outputs:
- token_diff: float32 [256, 16], P('dp')
- seq_diff: float32 [256], P('dp')
Inputs may be any that keep to these rules, and one draw needn't show every extreme that they name: `move_plan`: A permutation of the slots; slot // 16 is the owning index of dp, each owning exactly 16 requests; from one index of dp to one owner go either no requests or exactly 2.
All inputs are finite; a program needn't handle non-finite values. No bound on the sum of `lengths` on one device may be relied on, other than what follows from the above.
Results may differ from a plain program's by a relative error of at most 0.0081.
Values may be sent and summed in bfloat16 or wider, within the bound.
A program may use at most 64 MiB of HBM per device.

v0:
```python
import jax
import jax.numpy as jnp
from jax import lax
from jax.sharding import PartitionSpec as P

D = 2048
epsilon = 1e-05


def select_rows(selector, values):
    return jnp.dot(selector, values, preferred_element_type=jnp.float32).astype(jnp.bfloat16)


def norm_from_sums(values, first_sum, second_sum, gain, width):
    center = first_sum / width
    spread = second_sum / width - center * center
    return (values - center[:, None]) * lax.rsqrt(spread + epsilon)[:, None] * gain


def local(
    hidden_policy,
    hidden_reference,
    ffn_gain_policy,
    ffn_gain_reference,
    up_policy,
    up_reference,
    down_policy,
    down_reference,
    final_gain_policy,
    final_gain_reference,
    out_policy,
    out_reference,
    move_plan,
    lengths,
    targets,
):
    dp_count = lax.axis_size("dp")
    dp_index = lax.axis_index("dp")
    mp_index = lax.axis_index("mp")
    req_count = hidden_policy.shape[0]
    slot_count = hidden_policy.shape[1]
    width_part = hidden_policy.shape[2]
    tokens_here = req_count * slot_count
    capacity = max(2, req_count // min(8, dp_count))
    buffer_slots = dp_count * capacity
    plan = move_plan.reshape(dp_count, req_count)
    owner_device = plan // req_count
    positions = jnp.arange(req_count, dtype=jnp.int32)
    earlier = positions[None, :] < positions[:, None]
    same_owner = owner_device[:, :, None] == owner_device[:, None, :]
    rank = jnp.sum(jnp.logical_and(same_owner, earlier[None]), axis=2)
    own_owner = lax.dynamic_index_in_dim(owner_device, dp_index, 0, keepdims=False)
    own_rank = lax.dynamic_index_in_dim(rank, dp_index, 0, keepdims=False)
    send_slot = own_owner * capacity + own_rank
    send_select = (jnp.arange(buffer_slots, dtype=jnp.int32)[:, None] == send_slot[None, :]).astype(
        jnp.bfloat16
    )
    packed = (
        select_rows(send_select, hidden_policy.reshape(req_count, slot_count * width_part)),
        select_rows(send_select, hidden_reference.reshape(req_count, slot_count * width_part)),
    )
    arrived = (
        lax.all_to_all(packed[0], "dp", split_axis=0, concat_axis=0, tiled=True),
        lax.all_to_all(packed[1], "dp", split_axis=0, concat_axis=0, tiled=True),
    )
    column = jnp.arange(dp_count, dtype=jnp.int32)[:, None] * capacity + rank
    local_row = plan - dp_index * req_count
    owned = owner_device == dp_index
    row_hot = jnp.logical_and(
        local_row.reshape(-1)[:, None] == positions[None, :], owned.reshape(-1)[:, None]
    ).astype(jnp.bfloat16)
    column_hot = (
        column.reshape(-1)[:, None] == jnp.arange(buffer_slots, dtype=jnp.int32)[None, :]
    ).astype(jnp.bfloat16)
    receive_select = jnp.dot(row_hot.T, column_hot, preferred_element_type=jnp.float32).astype(
        jnp.bfloat16
    )
    moved_policy = select_rows(receive_select, arrived[0]).reshape(tokens_here, width_part)
    moved_reference = select_rows(receive_select, arrived[1]).reshape(tokens_here, width_part)
    stream_policy = moved_policy.astype(jnp.float32)
    stream_reference = moved_reference.astype(jnp.float32)
    ffn_sums = lax.psum(
        (
            jnp.sum(stream_policy, axis=1),
            jnp.sum(stream_policy * stream_policy, axis=1),
            jnp.sum(stream_reference, axis=1),
            jnp.sum(stream_reference * stream_reference, axis=1),
        ),
        "mp",
    )
    gain_policy_part = lax.dynamic_slice_in_dim(ffn_gain_policy, mp_index * width_part, width_part)
    gain_reference_part = lax.dynamic_slice_in_dim(
        ffn_gain_reference, mp_index * width_part, width_part
    )
    normed_policy = norm_from_sums(
        stream_policy, ffn_sums[0], ffn_sums[1], gain_policy_part, D
    ).astype(jnp.bfloat16)
    normed_reference = norm_from_sums(
        stream_reference, ffn_sums[2], ffn_sums[3], gain_reference_part, D
    ).astype(jnp.bfloat16)
    pieces = (
        lax.all_gather(normed_policy, "mp", axis=1, tiled=True),
        lax.all_gather(normed_reference, "mp", axis=1, tiled=True),
    )
    pre_policy = jnp.dot(pieces[0], up_policy, preferred_element_type=jnp.float32)
    pre_reference = jnp.dot(pieces[1], up_reference, preferred_element_type=jnp.float32)
    units_policy = jax.nn.gelu(pre_policy).astype(jnp.bfloat16)
    units_reference = jax.nn.gelu(pre_reference).astype(jnp.bfloat16)
    terms = (
        jnp.dot(units_policy, down_policy, preferred_element_type=jnp.float32),
        jnp.dot(units_reference, down_reference, preferred_element_type=jnp.float32),
    )
    summed = (
        lax.psum_scatter(terms[0], "mp", scatter_dimension=1, tiled=True),
        lax.psum_scatter(terms[1], "mp", scatter_dimension=1, tiled=True),
    )
    after_policy = stream_policy + summed[0]
    after_reference = stream_reference + summed[1]
    final_sums = lax.psum(
        (
            jnp.sum(after_policy, axis=1),
            jnp.sum(after_policy * after_policy, axis=1),
            jnp.sum(after_reference, axis=1),
            jnp.sum(after_reference * after_reference, axis=1),
        ),
        "mp",
    )
    final_policy_part = lax.dynamic_slice_in_dim(
        final_gain_policy, mp_index * width_part, width_part
    )
    final_reference_part = lax.dynamic_slice_in_dim(
        final_gain_reference, mp_index * width_part, width_part
    )
    out_normed_policy = norm_from_sums(
        after_policy, final_sums[0], final_sums[1], final_policy_part, D
    ).astype(jnp.bfloat16)
    out_normed_reference = norm_from_sums(
        after_reference, final_sums[2], final_sums[3], final_reference_part, D
    ).astype(jnp.bfloat16)
    full_policy, full_reference = (
        lax.all_gather(out_normed_policy, "mp", axis=1, tiled=True),
        lax.all_gather(out_normed_reference, "mp", axis=1, tiled=True),
    )
    vocab_part = out_policy.shape[1]
    pieces = (
        lax.all_gather(out_policy, "dp", axis=0, tiled=True),
        lax.all_gather(out_reference, "dp", axis=0, tiled=True),
    )
    logits_policy = jnp.dot(full_policy, pieces[0], preferred_element_type=jnp.float32)
    logits_reference = jnp.dot(full_reference, pieces[1], preferred_element_type=jnp.float32)
    wanted = targets.reshape(tokens_here)
    entry_ids = jnp.arange(vocab_part, dtype=jnp.int32)[None, :] + mp_index * vocab_part
    target_hit = entry_ids == wanted[:, None]
    picked_policy = jnp.sum(jnp.where(target_hit, logits_policy, 0.0), axis=1)
    picked_reference = jnp.sum(jnp.where(target_hit, logits_reference, 0.0), axis=1)
    top_policy, top_reference = lax.pmax(
        (jnp.max(logits_policy, axis=1), jnp.max(logits_reference, axis=1)), "mp"
    )
    totals = lax.psum(
        (
            jnp.sum(jnp.exp(logits_policy - top_policy[:, None]), axis=1),
            jnp.sum(jnp.exp(logits_reference - top_reference[:, None]), axis=1),
            picked_policy,
            picked_reference,
        ),
        "mp",
    )
    logprob_policy = totals[2] - (top_policy + jnp.log(totals[0]))
    logprob_reference = totals[3] - (top_reference + jnp.log(totals[1]))
    live = jnp.arange(slot_count, dtype=jnp.int32)[None, :] < lengths[:, None]
    token_diff = jnp.where(
        live, (logprob_policy - logprob_reference).reshape(req_count, slot_count), jnp.float32(0.0)
    )
    seq_diff = jnp.sum(token_diff, axis=1)
    return (token_diff, seq_diff)


def solution(mesh):
    return jax.shard_map(
        local,
        mesh=mesh,
        in_specs=(
            P("dp", None, "mp"),
            P("dp", None, "mp"),
            P(),
            P(),
            P(None, "mp"),
            P(None, "mp"),
            P("mp", None),
            P("mp", None),
            P(),
            P(),
            P("dp", "mp"),
            P("dp", "mp"),
            P(),
            P("dp"),
            P("dp", None),
        ),
        out_specs=(P("dp", None), P("dp")),
        check_vma=False,
    )
```

profile of v0, /device:TPU:1, one launch (start us, length us, event | category | flops | bytes accessed | tf_op | source)
XLA Modules:
  0.0 811.6 jit_solution(14091598724623640920)
XLA Ops:
  8.0 0.8 reshape.153
  8.9 1.0 reshape.155
  9.8 0.4 convert_reduce_fusion
  10.3 0.1 convolution_convert_fusion
  10.4 0.7 all_to_all.19
  11.1 7.6 all-to-all-start.1
  18.6 0.7 fusion.42
  19.3 0.7 broadcast_subtract_fusion
  20.2 1.0 reshape.154
  21.1 0.1 convolution_convert_fusion.1
  21.3 0.3 convolution_convert_fusion.4
  21.6 0.7 all_to_all.16
  22.2 0.8 dynamic_slice.23
  23.0 2.2 all-to-all-done.1
  25.2 4.5 all-to-all-start
  29.8 0.1 fusion
  29.9 0.1 reshape.158
  30.0 6.2 all-to-all-done
  36.2 0.1 fusion.1
  36.5 0.2 fusion.51
  36.8 54.5 %all-reduce.2 = (f32[256]{0:T(256)S(1)}, f32[256]{0:T(256)S(1)}, f32[256]{0:T(256)S(1)}, f32[256]{0:T(256)S(1)}) all-reduce(f32[256]{0:T(256)S(1)} %get-tuple-element.46, f32[256]{0:T(256)S(1)} %get-tuple-element.47, f32[256]{0:T(256)S(1)} %get-tuple-element.7, f32[256]{0:T(256)S(1)} %get-tuple-element.6), channel_id=1, replica_groups=mesh['dp'=16,'mp'=32] {'mp'}, use_global_device_ids=true, to_apply=%region_19.20 | all-reduce | flops 1024 | bytes 8192 | tf_op jit(solution)/shard_map/psum | solution.py:82
  91.2 0.7 multiply_convert_fusion.1
  92.0 0.8 dynamic_slice.21
  92.9 0.7 multiply_convert_fusion.3
  93.6 63.8 %all-gather.13.cloned.1.call-done = bf16[256,2048]{0,1:T(8,128)(2,1)} async-done(((bf16[256,64]{0,1:T(8,128)(2,1)}), bf16[256,2048]{0,1:T(8,128)(2,1)}) %all-gather.13.cloned.1.call-update) | async-done | bytes 1048592 | tf_op jit(solution)/shard_map/all_gather | solution.py:103
  157.4 3.6 fusion.22
  161.1 66.3 %all-gather.7.cloned.1.call-done = bf16[256,2048]{0,1:T(8,128)(2,1)} async-done(((bf16[256,64]{0,1:T(8,128)(2,1)}), bf16[256,2048]{0,1:T(8,128)(2,1)}) %all-gather.7.cloned.1.call-update) | async-done | bytes 1048592 | tf_op jit(solution)/shard_map/all_gather | solution.py:102
  227.4 3.4 fusion.24
  230.9 0.5 all-gather.17.cloned.1.call-update
  231.5 0.8 dynamic_slice.24
  232.2 102.6 %reduce-scatter.5.cloned.1.call-done = f32[256,64]{0,1:T(8,128)} async-done(((f32[256,2048]{0,1:T(8,128)}), f32[256,64]{0,1:T(8,128)}) %reduce-scatter.5.cloned.1.call-update) | async-done | bytes 65552 | tf_op jit(solution)/shard_map/reduce_scatter | solution.py:115
  334.9 0.9 fusion.54
  335.7 109.6 %reduce-scatter.3.cloned.1.call-done = f32[256,64]{0,1:T(8,128)} async-done(((f32[256,2048]{0,1:T(8,128)}), f32[256,64]{0,1:T(8,128)}) %reduce-scatter.3.cloned.1.call-update) | async-done | bytes 65552 | tf_op jit(solution)/shard_map/reduce_scatter | solution.py:114
  445.4 0.9 fusion.53
  446.2 48.8 %all-reduce.1 = (f32[256]{0:T(256)S(1)}, f32[256]{0:T(256)S(1)}, f32[256]{0:T(256)S(1)}, f32[256]{0:T(256)S(1)}) all-reduce(f32[256]{0:T(256)S(1)} %get-tuple-element.13, f32[256]{0:T(256)S(1)} %get-tuple-element.12, f32[256]{0:T(256)S(1)} %get-tuple-element.11, f32[256]{0:T(256)S(1)} %get-tuple-element.10), channel_id=1, replica_groups=mesh['dp'=16,'mp'=32] {'mp'}, use_global_device_ids=true, to_apply=%region_24.25 | all-reduce | flops 1024 | bytes 8192 | tf_op jit(solution)/shard_map/psum | solution.py:119
  495.0 0.7 multiply_convert_fusion
  495.8 0.5 all-gather.11.cloned.1.call-update
  496.4 0.8 dynamic_slice.22
  497.1 0.7 multiply_convert_fusion.2
  498.0 69.6 %all-gather.15.cloned.1.call-done = bf16[256,2048]{0,1:T(8,128)(2,1)} async-done(((bf16[256,64]{0,1:T(8,128)(2,1)}), bf16[256,2048]{0,1:T(8,128)(2,1)}) %all-gather.15.cloned.1.call-update) | async-done | bytes 1048592 | tf_op jit(solution)/shard_map/all_gather | solution.py:142
  567.6 3.7 fusion.57
  571.3 60.5 %all-gather.11.cloned.1.call-done = bf16[2048,896]{1,0:T(8,128)(2,1)} async-done(((bf16[128,896]{1,0:T(8,128)(2,1)}), bf16[2048,896]{1,0:T(8,128)(2,1)}) %all-gather.11.cloned.1.call-update) | async-done | bytes 3670032 | tf_op jit(solution)/shard_map/all_gather | solution.py:146
  631.8 73.1 %all-gather.9.cloned.1.call-done = bf16[256,2048]{0,1:T(8,128)(2,1)} async-done(((bf16[256,64]{0,1:T(8,128)(2,1)}), bf16[256,2048]{0,1:T(8,128)(2,1)}) %all-gather.9.cloned.1.call-update) | async-done | bytes 1048592 | tf_op jit(solution)/shard_map/all_gather | solution.py:141
  704.9 3.7 fusion.58
  708.6 45.4 %all-reduce.3 = (f32[256]{0:T(256)S(1)}, f32[256]{0:T(256)S(1)}) all-reduce(f32[256]{0:T(256)S(1)} %get-tuple-element.42, f32[256]{0:T(256)S(1)} %get-tuple-element.44), channel_id=1, replica_groups=mesh['dp'=16,'mp'=32] {'mp'}, use_global_device_ids=true, to_apply=%region_28.29 | all-reduce | flops 512 | bytes 4096 | tf_op jit(solution)/shard_map/pmax | solution.py:156
  754.0 0.6 exponential_reduce_fusion.1
  754.6 48.2 %all-reduce = (f32[256]{0:T(256)S(1)}, f32[256]{0:T(256)S(1)}, f32[256]{0:T(256)S(1)}, f32[256]{0:T(256)S(1)}) all-reduce(f32[256]{0:T(256)S(1)} %get-tuple-element.32, f32[256]{0:T(256)S(1)} %get-tuple-element.33, f32[256]{0:T(256)S(1)} %get-tuple-element.3, f32[256]{0:T(256)S(1)} %get-tuple-element.2), channel_id=1, replica_groups=mesh['dp'=16,'mp'=32] {'mp'}, use_global_device_ids=true, to_apply=%region_26.27 | all-reduce | flops 1024 | bytes 8192 | tf_op jit(solution)/shard_map/psum | solution.py:159
  802.9 1.3 fusion.55
  (44 shorter events, 1.2 us)
Async XLA Ops:
  8.0 149.4 %copy-start = (bf16[128,2048]{1,0:T(8,128)(2,1)S(1)}, bf16[128,2048]{1,0:T(8,128)(2,1)}, u32[]{:S(2)}) copy-start(bf16[128,2048]{1,0:T(8,128)(2,1)} %param.22) | copy-start | bytes 1572868
  11.1 14.1 %all-to-all-start.1 = ((bf16[16,2,1024]{2,1,0:T(2,128)(2,1)}), bf16[16,2,1024]{2,1,0:T(2,128)(2,1)S(1)}, u32[]{:S(2)}, u32[]{:S(2)}) async-start(bf16[16,2,1024]{2,1,0:T(2,128)(2,1)} %all_to_all.19), calls=%async_computation.2 | async-start | bytes 131072 | tf_op jit(solution)/shard_map/all_to_all | solution.py:64
  25.2 11.0 %all-to-all-start = ((bf16[16,2,1024]{2,1,0:T(2,128)(2,1)}), bf16[16,2,1024]{2,1,0:T(2,128)(2,1)S(1)}, u32[]{:S(2)}, u32[]{:S(2)}) async-start(bf16[16,2,1024]{2,1,0:T(2,128)(2,1)} %all_to_all.16), calls=%async_computation | async-start | bytes 131072 | tf_op jit(solution)/shard_map/all_to_all | solution.py:63
  29.7 127.7 %all-gather.13.cloned.1.call-start = ((), (), s32[]{:S(2)}) async-start(), calls=%async_computation.8 | async-start | bytes 1081344 | tf_op jit(solution)/shard_map/all_gather | solution.py:103
  36.4 190.9 %copy-start.1 = (bf16[128,2048]{1,0:T(8,128)(2,1)S(1)}, bf16[128,2048]{1,0:T(8,128)(2,1)}, u32[]{:S(2)}) copy-start(bf16[128,2048]{1,0:T(8,128)(2,1)} %param.21) | copy-start | bytes 1572868
  36.4 190.9 %copy-start.2 = (bf16[2048,128]{1,0:T(8,128)(2,1)S(1)}, bf16[2048,128]{1,0:T(8,128)(2,1)}, u32[]{:S(2)}) copy-start(bf16[2048,128]{1,0:T(8,128)(2,1)} %param.19) | copy-start | bytes 1572868
  92.0 135.4 %all-gather.7.cloned.1.call-start = ((), (), s32[]{:S(2)}) async-start(), calls=%async_computation.4 | async-start | bytes 1081344 | tf_op jit(solution)/shard_map/all_gather | solution.py:102
  93.6 241.3 %reduce-scatter.5.cloned.1.call-start = ((), (), s32[]{:S(2)}) async-start(), calls=%async_computation.9 | async-start | bytes 2162688 | tf_op jit(solution)/shard_map/reduce_scatter | solution.py:115
  161.0 336.8 %copy-start.3 = (s32[16,16]{1,0:T(8,128)S(1)}, s32[16,16]{1,0:T(8,128)}, u32[]{:S(2)}) copy-start(s32[16,16]{1,0:T(8,128)} %param.29) | copy-start | bytes 3076
  161.0 284.3 %reduce-scatter.3.cloned.1.call-start = ((), (), s32[]{:S(2)}) async-start(), calls=%async_computation.5 | async-start | bytes 2162688 | tf_op jit(solution)/shard_map/reduce_scatter | solution.py:114
  230.8 267.1 %all-gather.17.cloned.1.call-start = ((), (), s32[]{:S(2)}) async-start(), calls=%async_computation.11 | async-start | bytes 3899392 | tf_op jit(solution)/shard_map/all_gather | solution.py:147
  231.4 336.2 %all-gather.15.cloned.1.call-start = ((), (), s32[]{:S(2)}) async-start(), calls=%async_computation.10 | async-start | bytes 1081344 | tf_op jit(solution)/shard_map/all_gather | solution.py:142
  495.7 136.1 %all-gather.11.cloned.1.call-start = ((), (), s32[]{:S(2)}) async-start(), calls=%async_computation.7 | async-start | bytes 3899392 | tf_op jit(solution)/shard_map/all_gather | solution.py:146
  496.3 208.6 %all-gather.9.cloned.1.call-start = ((), (), s32[]{:S(2)}) async-start(), calls=%async_computation.6 | async-start | bytes 1081344 | tf_op jit(solution)/shard_map/all_gather | solution.py:141
  571.3 231.6 %copy-start.4 = (s32[16]{0:T(128)S(1)}, s32[16]{0:T(128)}, u32[]{:S(2)}) copy-start(s32[16]{0:T(128)} %param.28) | copy-start | bytes 196
Sparse Core Ops, SparseCore 0:
  92.1 65.2 all-gather.12
  159.5 67.8 all-gather.6
  230.2 104.6 reduce-scatter.4
  337.8 107.5 reduce-scatter.2
Sparse Core Ops, SparseCore 1:
  234.4 61.3 all-gather.16
  495.8 71.7 all-gather.14
  570.5 61.2 all-gather.10
  633.9 70.9 all-gather.8
where the time goes:
time: 812 us
  waiting for transfers between devices  555 us (68%)
  blocking collectives  197 us (24%)
  between operations  15.6 us (2%)
  matrix products  15.3 us (2%)
  starting transfers between devices  12.4 us (2%)
  other arithmetic  8.56 us (1%)
    reduce_scatter x1, waiting for transfers between devices, local(): lax.psum_scatter(terms[0], 'mp', scatter_dimension=1, tiled=True)  110 us
    reduce_scatter x1, waiting for transfers between devices, local(): lax.psum_scatter(terms[1], 'mp', scatter_dimension=1, tiled=True)  103 us
    all_gather x1, waiting for transfers between devices, local(): lax.all_gather(out_normed_policy, 'mp', axis=1, tiled=True)  73.1 us
    all_gather x1, waiting for transfers between devices, local(): lax.all_gather(out_normed_reference, 'mp', axis=1, tiled=True)  69.6 us
    all_gather x1, waiting for transfers between devices, local(): lax.all_gather(normed_policy, 'mp', axis=1, tiled=True)  66.3 us
    all_gather x1, waiting for transfers between devices, local(): lax.all_gather(normed_reference, 'mp', axis=1, tiled=True)  63.8 us
    all_gather x1, waiting for transfers between devices, local(): lax.all_gather(out_policy, 'dp', axis=0, tiled=True)  60.5 us
    psum x1, blocking collectives, local(): lax.psum((jnp.sum(stream_policy, axis=1), jnp.sum(stream_policy * stream_...  54.5 us
  transfers between devices with their start and end apart: 10, of which 9 were waited for; matrix products, arithmetic and copies ran while one was open for 3% of the time, Pallas kernels for 0%

commit v1 on v0

--- a/solution.py
+++ b/solution.py
@@ -5,6 +5,19 @@
 
 D = 2048
 epsilon = 1e-05
+
+
+def collect(value, axis, dim):
+    ways = lax.axis_size(axis)
+    up = [(d, (d + 1) % ways) for d in range(ways)]
+    down = [(d, (d - 1) % ways) for d in range(ways)]
+    earlier, later = ([value], [value])
+    for _ in range(ways // 2):
+        earlier.append(lax.ppermute(earlier[-1], axis, up))
+    for _ in range((ways - 1) // 2):
+        later.append(lax.ppermute(later[-1], axis, down))
+    line = jnp.concatenate([*earlier[::-1], *later[1:]], axis=dim)
+    return jnp.roll(line, (lax.axis_index(axis) - ways // 2) * value.shape[dim], axis=dim)
 
 
 def select_rows(selector, values):
@@ -142,10 +155,7 @@
         lax.all_gather(out_normed_reference, "mp", axis=1, tiled=True),
     )
     vocab_part = out_policy.shape[1]
-    pieces = (
-        lax.all_gather(out_policy, "dp", axis=0, tiled=True),
-        lax.all_gather(out_reference, "dp", axis=0, tiled=True),
-    )
+    pieces = (collect(out_policy, "dp", 0), lax.all_gather(out_reference, "dp", axis=0, tiled=True))
     logits_policy = jnp.dot(full_policy, pieces[0], preferred_element_type=jnp.float32)
     logits_reference = jnp.dot(full_reference, pieces[1], preferred_element_type=jnp.float32)
     wanted = targets.reshape(tokens_here)

time: 812 us -> 748 us (0.921)
  waiting for transfers between devices: 555 us -> 395 us
  starting transfers between devices: 12.4 us -> 76.8 us
  local copies, waits for them, and re-layouts: 7.74 us -> 36.2 us
    reduce_scatter x1, waiting for transfers between devices: 103 us -> 9.06 us  [local(): lax.psum_scatter(terms[1], 'mp', scatter_dimension=1, tiled=True)]
    ppermute x0 -> x15, starting transfers between devices: none -> 64.4 us  [the longest x7 47.9 us: collect(): later.append(lax.ppermute(later[-1], axis, down))]
    all_gather x1 -> x0, waiting for transfers between devices: 60.5 us -> none  [local(): lax.all_gather(out_policy, 'dp', axis=0, tiled=True)]
    unnamed x10 -> x47, local copies, waits for them, and re-layouts: 0.03 us -> 26.8 us
    ppermute x0 -> x15, waiting for transfers between devices: none -> 24.8 us  [the longest x8 21.6 us: collect(): earlier.append(lax.ppermute(earlier[-1], axis, up))]
    all_gather x1, waiting for transfers between devices: 69.6 us -> 46.5 us  [local(): lax.all_gather(out_normed_reference, 'mp', axis=1, tiled=True)]
  transfers between devices with their start and end apart: 10 -> 24, of which waited for: 9 -> 18; matrix products, arithmetic and copies ran while one was open for 3% -> 7% of each run, Pallas kernels for 0% -> 0%
where the time goes in v1:
time: 748 us; the launch traced here: 747 us
  waiting for transfers between devices  395 us (53%)
  blocking collectives  197 us (26%)
  starting transfers between devices  76.8 us (10%)
  local copies, waits for them, and re-layouts  36.2 us (5%)
  between operations  15.8 us (2%)
  matrix products  15.3 us (2%)
  other arithmetic  11.5 us (2%)
    reduce_scatter x1, waiting for transfers between devices, local(): lax.psum_scatter(terms[0], 'mp', scatter_dimension=1, tiled=True)  109 us
    all_gather x1, waiting for transfers between devices, local(): lax.all_gather(out_normed_policy, 'mp', axis=1, tiled=True)  66.3 us
    all_gather x1, waiting for transfers between devices, local(): lax.all_gather(normed_policy, 'mp', axis=1, tiled=True)  66.3 us
    all_gather x1, waiting for transfers between devices, local(): lax.all_gather(normed_reference, 'mp', axis=1, tiled=True)  63.7 us
    psum x1, blocking collectives, local(): lax.psum((jnp.sum(stream_policy, axis=1), jnp.sum(stream_policy * stream_...  54.5 us
    psum x1, blocking collectives, local(): lax.psum((jnp.sum(after_policy, axis=1), jnp.sum(after_policy * after_pol...  48.8 us
    psum x1, blocking collectives, local(): lax.psum((jnp.sum(jnp.exp(logits_policy - top_policy[:, None]), axis=1),...  48.2 us
    ppermute x7, starting transfers between devices, collect(): later.append(lax.ppermute(later[-1], axis, down))  47.9 us
  transfers between devices with their start and end apart: 24, of which 18 were waited for; matrix products, arithmetic and copies ran while one was open for 7% of the time, Pallas kernels for 0%

profile of v1, /device:TPU:1, one launch (start us, length us, event | category | flops | bytes accessed | tf_op | source)
XLA Modules:
  0.0 747.1 jit_solution(8465855087028428129)
XLA Ops:
  11.1 7.6 %all-to-all-start.1 = ((bf16[16,2,1024]{2,1,0:T(2,128)(2,1)}), bf16[16,2,1024]{2,1,0:T(2,128)(2,1)S(1)}, u32[]{:S(2)}, u32[]{:S(2)}) async-start(bf16[16,2,1024]{2,1,0:T(2,128)(2,1)} %all_to_all.19), calls=%async_computation.2 | async-start | bytes 131072 | tf_op jit(solution)/shard_map/all_to_all | solution.py:77
  23.1 2.2 all-to-all-done.1
  25.2 4.5 all-to-all-start
  30.1 6.2 all-to-all-done
  36.8 54.5 %all-reduce.2 = (f32[256]{0:T(256)S(1)}, f32[256]{0:T(256)S(1)}, f32[256]{0:T(256)S(1)}, f32[256]{0:T(256)S(1)}) all-reduce(f32[256]{0:T(256)S(1)} %get-tuple-element.46, f32[256]{0:T(256)S(1)} %get-tuple-element.47, f32[256]{0:T(256)S(1)} %get-tuple-element.7, f32[256]{0:T(256)S(1)} %get-tuple-element.6), channel_id=1, replica_groups=mesh['dp'=16,'mp'=32] {'mp'}, use_global_device_ids=true, to_apply=%region_19.20 | all-reduce | flops 1024 | bytes 8192 | tf_op jit(solution)/shard_map/psum | solution.py:95
  93.7 63.7 %all-gather.10.cloned.1.call-done = bf16[256,2048]{0,1:T(8,128)(2,1)} async-done(((bf16[256,64]{0,1:T(8,128)(2,1)}), bf16[256,2048]{0,1:T(8,128)(2,1)}) %all-gather.10.cloned.1.call-update) | async-done | bytes 1048592 | tf_op jit(solution)/shard_map/all_gather | solution.py:116
  157.5 3.6 fusion.24
  161.1 66.3 %all-gather.6.cloned.1.call-done = bf16[256,2048]{0,1:T(8,128)(2,1)} async-done(((bf16[256,64]{0,1:T(8,128)(2,1)}), bf16[256,2048]{0,1:T(8,128)(2,1)}) %all-gather.6.cloned.1.call-update) | async-done | bytes 1048592 | tf_op jit(solution)/shard_map/all_gather | solution.py:115
  227.4 3.5 fusion.26
  231.6 3.1 collective-permute-start
  234.7 9.0 %collective-permute-done = bf16[128,896]{1,0:T(8,128)(2,1)S(1)} collective-permute-done((bf16[128,896]{1,0:T(8,128)(2,1)S(1)}, bf16[128,896]{1,0:T(8,128)(2,1)S(1)}, u32[]{:S(2)}, u32[]{:S(2)}) %collective-permute-start) | collective-permute-done | bytes 229408 | tf_op jit(solution)/shard_map/ppermute | solution.py:16
  243.7 1.9 collective-permute-start.1
  245.6 6.7 collective-permute-start.8
  252.3 2.6 collective-permute-done.1
  254.9 1.9 collective-permute-start.2
  256.8 6.9 collective-permute-start.9
  263.7 2.2 collective-permute-done.2
  265.9 1.9 collective-permute-start.3
  267.8 6.7 collective-permute-start.10
  276.0 1.9 collective-permute-start.4
  277.9 6.7 collective-permute-start.11
  284.6 1.6 collective-permute-done.4
  286.1 1.9 collective-permute-start.5
  288.1 2.9 collective-permute-done.11
  290.9 7.1 collective-permute-start.12
  298.1 3.8 collective-permute-done.5
  301.9 1.9 collective-permute-start.6
  304.1 7.2 collective-permute-start.13
  312.1 1.9 collective-permute-start.7
  315.7 6.7 collective-permute-start.14
  322.5 1.6 constant_dynamic-update-slice_fusion.31
  324.1 1.7 constant_dynamic-update-slice_fusion.30
  327.2 9.1 %reduce-scatter.5.cloned.1.call-done = f32[256,64]{0,1:T(8,128)} async-done(((f32[256,2048]{0,1:T(8,128)}), f32[256,64]{0,1:T(8,128)}) %reduce-scatter.5.cloned.1.call-update) | async-done | bytes 65552 | tf_op jit(solution)/shard_map/reduce_scatter | solution.py:128
  336.3 1.5 fusion.60
  337.8 108.9 %reduce-scatter.3.cloned.1.call-done = f32[256,64]{0,1:T(8,128)} async-done(((f32[256,2048]{0,1:T(8,128)}), f32[256,64]{0,1:T(8,128)}) %reduce-scatter.3.cloned.1.call-update) | async-done | bytes 65552 | tf_op jit(solution)/shard_map/reduce_scatter | solution.py:127
  448.2 48.8 %all-reduce.1 = (f32[256]{0:T(256)S(1)}, f32[256]{0:T(256)S(1)}, f32[256]{0:T(256)S(1)}, f32[256]{0:T(256)S(1)}) all-reduce(f32[256]{0:T(256)S(1)} %get-tuple-element.13, f32[256]{0:T(256)S(1)} %get-tuple-element.12, f32[256]{0:T(256)S(1)} %get-tuple-element.11, f32[256]{0:T(256)S(1)} %get-tuple-element.10), channel_id=1, replica_groups=mesh['dp'=16,'mp'=32] {'mp'}, use_global_device_ids=true, to_apply=%region_24.25 | all-reduce | flops 1024 | bytes 8192 | tf_op jit(solution)/shard_map/psum | solution.py:132
  497.0 1.5 multiply_convert_fusion
  506.4 1.7 constant_dynamic-update-slice_fusion.16
  508.1 1.6 constant_dynamic-update-slice_fusion.15
  509.7 1.7 constant_dynamic-update-slice_fusion.14
  511.4 1.5 multiply_convert_fusion.2
  522.2 1.7 constant_dynamic-update-slice_fusion
  523.8 46.5 %all-gather.12.cloned.1.call-done = bf16[256,2048]{0,1:T(8,128)(2,1)} async-done(((bf16[256,64]{0,1:T(8,128)(2,1)}), bf16[256,2048]{0,1:T(8,128)(2,1)}) %all-gather.12.cloned.1.call-update) | async-done | bytes 1048592 | tf_op jit(solution)/shard_map/all_gather | solution.py:155
  570.3 3.7 fusion.63
  574.1 66.3 %all-gather.8.cloned.1.call-done = bf16[256,2048]{0,1:T(8,128)(2,1)} async-done(((bf16[256,64]{0,1:T(8,128)(2,1)}), bf16[256,2048]{0,1:T(8,128)(2,1)}) %all-gather.8.cloned.1.call-update) | async-done | bytes 1048592 | tf_op jit(solution)/shard_map/all_gather | solution.py:154
  640.4 3.7 fusion.64
  644.1 45.4 %all-reduce.3 = (f32[256]{0:T(256)S(1)}, f32[256]{0:T(256)S(1)}) all-reduce(f32[256]{0:T(256)S(1)} %get-tuple-element.42, f32[256]{0:T(256)S(1)} %get-tuple-element.44), channel_id=1, replica_groups=mesh['dp'=16,'mp'=32] {'mp'}, use_global_device_ids=true, to_apply=%region_28.29 | all-reduce | flops 512 | bytes 4096 | tf_op jit(solution)/shard_map/pmax | solution.py:166
  690.2 48.2 %all-reduce = (f32[256]{0:T(256)S(1)}, f32[256]{0:T(256)S(1)}, f32[256]{0:T(256)S(1)}, f32[256]{0:T(256)S(1)}) all-reduce(f32[256]{0:T(256)S(1)} %get-tuple-element.32, f32[256]{0:T(256)S(1)} %get-tuple-element.33, f32[256]{0:T(256)S(1)} %get-tuple-element.3, f32[256]{0:T(256)S(1)} %get-tuple-element.2), channel_id=1, replica_groups=mesh['dp'=16,'mp'=32] {'mp'}, use_global_device_ids=true, to_apply=%region_26.27 | all-reduce | flops 1024 | bytes 8192 | tf_op jit(solution)/shard_map/psum | solution.py:169
  (109 shorter events, 37.7 us)
Async XLA Ops:
  8.0 149.5 %copy-start = (bf16[128,2048]{1,0:T(8,128)(2,1)S(1)}, bf16[128,2048]{1,0:T(8,128)(2,1)}, u32[]{:S(2)}) copy-start(bf16[128,2048]{1,0:T(8,128)(2,1)} %param.22) | copy-start | bytes 1572868
  8.0 219.4 %copy-start.5 = (bf16[2048,128]{1,0:T(8,128)(2,1)S(1)}, bf16[2048,128]{1,0:T(8,128)(2,1)}, u32[]{:S(2)}) copy-start(bf16[2048,128]{1,0:T(8,128)(2,1)} %param.19) | copy-start | bytes 1572868
  8.0 219.4 %copy-start.4 = (bf16[128,2048]{1,0:T(8,128)(2,1)S(1)}, bf16[128,2048]{1,0:T(8,128)(2,1)}, u32[]{:S(2)}) copy-start(bf16[128,2048]{1,0:T(8,128)(2,1)} %param.21) | copy-start | bytes 1572868
  11.1 14.1 %all-to-all-start.1 = ((bf16[16,2,1024]{2,1,0:T(2,128)(2,1)}), bf16[16,2,1024]{2,1,0:T(2,128)(2,1)S(1)}, u32[]{:S(2)}, u32[]{:S(2)}) async-start(bf16[16,2,1024]{2,1,0:T(2,128)(2,1)} %all_to_all.19), calls=%async_computation.2 | async-start | bytes 131072 | tf_op jit(solution)/shard_map/all_to_all | solution.py:77
  25.2 11.0 %all-to-all-start = ((bf16[16,2,1024]{2,1,0:T(2,128)(2,1)}), bf16[16,2,1024]{2,1,0:T(2,128)(2,1)S(1)}, u32[]{:S(2)}, u32[]{:S(2)}) async-start(bf16[16,2,1024]{2,1,0:T(2,128)(2,1)} %all_to_all.16), calls=%async_computation | async-start | bytes 131072 | tf_op jit(solution)/shard_map/all_to_all | solution.py:76
  29.8 201.8 %copy-start.1 = (bf16[128,896]{1,0:T(8,128)(2,1)S(1)}, bf16[128,896]{1,0:T(8,128)(2,1)}, u32[]{:S(2)}) copy-start(bf16[128,896]{1,0:T(8,128)(2,1)} %param.25) | copy-start | bytes 688132
  29.8 127.7 %all-gather.10.cloned.1.call-start = ((), (), s32[]{:S(2)}) async-start(), calls=%async_computation.7 | async-start | bytes 1081344 | tf_op jit(solution)/shard_map/all_gather | solution.py:116
  29.9 285.7 %copy-start.6 = (s32[16,16]{1,0:T(8,128)S(1)}, s32[16,16]{1,0:T(8,128)}, u32[]{:S(2)}) copy-start(s32[16,16]{1,0:T(8,128)} %param.29) | copy-start | bytes 3076
  36.6 207.1 %copy-start.2 = (f32[256,64]{0,1:T(8,128)}, f32[256,64]{0,1:T(8,128)S(1)}, u32[]{:S(2)}) copy-start(f32[256,64]{0,1:T(8,128)S(1)} %copy.32) | copy-start | bytes 196612
  92.0 135.4 %all-gather.6.cloned.1.call-start = ((), (), s32[]{:S(2)}) async-start(), calls=%async_computation.4 | async-start | bytes 1081344 | tf_op jit(solution)/shard_map/all_gather | solution.py:115
  92.9 138.6 %copy-start.3 = (f32[256,64]{0,1:T(8,128)}, f32[256,64]{0,1:T(8,128)S(1)}, u32[]{:S(2)}) copy-start(f32[256,64]{0,1:T(8,128)S(1)} %copy.30) | copy-start | bytes 196612
  93.7 242.6 %reduce-scatter.5.cloned.1.call-start = ((), (), s32[]{:S(2)}) async-start(), calls=%async_computation.8 | async-start | bytes 2162688 | tf_op jit(solution)/shard_map/reduce_scatter | solution.py:128
  161.1 285.6 %reduce-scatter.3.cloned.1.call-start = ((), (), s32[]{:S(2)}) async-start(), calls=%async_computation.5 | async-start | bytes 2162688 | tf_op jit(solution)/shard_map/reduce_scatter | solution.py:127
  230.9 292.9 %all-gather.14.cloned.1.call-start = ((), (), s32[]{:S(2)}) async-start(), calls=%async_computation.10 | async-start | bytes 3899392 | tf_op jit(solution)/shard_map/all_gather | solution.py:158
  231.5 338.8 %all-gather.12.cloned.1.call-start = ((), (), s32[]{:S(2)}) async-start(), calls=%async_computation.9 | async-start | bytes 1081344 | tf_op jit(solution)/shard_map/all_gather | solution.py:155
  231.6 12.1 %collective-permute-start = (bf16[128,896]{1,0:T(8,128)(2,1)S(1)}, bf16[128,896]{1,0:T(8,128)(2,1)S(1)}, u32[]{:S(2)}, u32[]{:S(2)}) collective-permute-start(bf16[128,896]{1,0:T(8,128)(2,1)S(1)} %copy-done.1), channel_id=1, source_target_pairs={{0,32},{32,64},{64,96},{96,128},{128,160},{160,192},{192,224},{224... | collective-permute-start | bytes 688136 | tf_op jit(solution)/shard_map/ppermute | solution.py:16
  243.7 11.2 %collective-permute-start.1 = (bf16[128,896]{1,0:T(8,128)(2,1)S(1)}, bf16[128,896]{1,0:T(8,128)(2,1)S(1)}, u32[]{:S(2)}, u32[]{:S(2)}) collective-permute-start(bf16[128,896]{1,0:T(8,128)(2,1)S(1)} %collective-permute-done), channel_id=1, source_target_pairs={{0,32},{32,64},{64,96},{96,128},{128,160},{160,192},{192,224},{224... | collective-permute-start | bytes 688136 | tf_op jit(solution)/shard_map/ppermute | solution.py:16
  245.6 11.2 %collective-permute-start.8 = (bf16[128,896]{1,0:T(8,128)(2,1)S(1)}, bf16[128,896]{1,0:T(8,128)(2,1)S(1)}, u32[]{:S(2)}, u32[]{:S(2)}) collective-permute-start(bf16[128,896]{1,0:T(8,128)(2,1)S(1)} %copy-done.1), channel_id=1, source_target_pairs={{0,480},{32,0},{64,32},{96,64},{128,96},{160,128},{192,160},{224,1... | collective-permute-start | bytes 688136 | tf_op jit(solution)/shard_map/ppermute | solution.py:18
  254.9 11.0 %collective-permute-start.2 = (bf16[128,896]{1,0:T(8,128)(2,1)S(1)}, bf16[128,896]{1,0:T(8,128)(2,1)S(1)}, u32[]{:S(2)}, u32[]{:S(2)}) collective-permute-start(bf16[128,896]{1,0:T(8,128)(2,1)S(1)} %collective-permute-done.1), channel_id=1, source_target_pairs={{0,32},{32,64},{64,96},{96,128},{128,160},{160,192},{192,224},{224... | collective-permute-start | bytes 688136 | tf_op jit(solution)/shard_map/ppermute | solution.py:16
  256.8 11.0 %collective-permute-start.9 = (bf16[128,896]{1,0:T(8,128)(2,1)S(1)}, bf16[128,896]{1,0:T(8,128)(2,1)S(1)}, u32[]{:S(2)}, u32[]{:S(2)}) collective-permute-start(bf16[128,896]{1,0:T(8,128)(2,1)S(1)} %collective-permute-done.8), channel_id=1, source_target_pairs={{0,480},{32,0},{64,32},{96,64},{128,96},{160,128},{192,160},{224,1... | collective-permute-start | bytes 688136 | tf_op jit(solution)/shard_map/ppermute | solution.py:18
  265.9 10.1 %collective-permute-start.3 = (bf16[128,896]{1,0:T(8,128)(2,1)S(1)}, bf16[128,896]{1,0:T(8,128)(2,1)S(1)}, u32[]{:S(2)}, u32[]{:S(2)}) collective-permute-start(bf16[128,896]{1,0:T(8,128)(2,1)S(1)} %collective-permute-done.2), channel_id=1, source_target_pairs={{0,32},{32,64},{64,96},{96,128},{128,160},{160,192},{192,224},{224... | collective-permute-start | bytes 688136 | tf_op jit(solution)/shard_map/ppermute | solution.py:16
  267.8 10.1 %collective-permute-start.10 = (bf16[128,896]{1,0:T(8,128)(2,1)S(1)}, bf16[128,896]{1,0:T(8,128)(2,1)S(1)}, u32[]{:S(2)}, u32[]{:S(2)}) collective-permute-start(bf16[128,896]{1,0:T(8,128)(2,1)S(1)} %collective-permute-done.9), channel_id=1, source_target_pairs={{0,480},{32,0},{64,32},{96,64},{128,96},{160,128},{192,160},{224,1... | collective-permute-start | bytes 688136 | tf_op jit(solution)/shard_map/ppermute | solution.py:18
  276.0 10.2 %collective-permute-start.4 = (bf16[128,896]{1,0:T(8,128)(2,1)S(1)}, bf16[128,896]{1,0:T(8,128)(2,1)S(1)}, u32[]{:S(2)}, u32[]{:S(2)}) collective-permute-start(bf16[128,896]{1,0:T(8,128)(2,1)S(1)} %collective-permute-done.3), channel_id=1, source_target_pairs={{0,32},{32,64},{64,96},{96,128},{128,160},{160,192},{192,224},{224... | collective-permute-start | bytes 688136 | tf_op jit(solution)/shard_map/ppermute | solution.py:16
  277.9 13.0 %collective-permute-start.11 = (bf16[128,896]{1,0:T(8,128)(2,1)S(1)}, bf16[128,896]{1,0:T(8,128)(2,1)S(1)}, u32[]{:S(2)}, u32[]{:S(2)}) collective-permute-start(bf16[128,896]{1,0:T(8,128)(2,1)S(1)} %collective-permute-done.10), channel_id=1, source_target_pairs={{0,480},{32,0},{64,32},{96,64},{128,96},{160,128},{192,160},{224,1... | collective-permute-start | bytes 688136 | tf_op jit(solution)/shard_map/ppermute | solution.py:18
  286.1 15.8 %collective-permute-start.5 = (bf16[128,896]{1,0:T(8,128)(2,1)S(1)}, bf16[128,896]{1,0:T(8,128)(2,1)S(1)}, u32[]{:S(2)}, u32[]{:S(2)}) collective-permute-start(bf16[128,896]{1,0:T(8,128)(2,1)S(1)} %collective-permute-done.4), channel_id=1, source_target_pairs={{0,32},{32,64},{64,96},{96,128},{128,160},{160,192},{192,224},{224... | collective-permute-start | bytes 688136 | tf_op jit(solution)/shard_map/ppermute | solution.py:16
  290.9 13.2 %collective-permute-start.12 = (bf16[128,896]{1,0:T(8,128)(2,1)S(1)}, bf16[128,896]{1,0:T(8,128)(2,1)S(1)}, u32[]{:S(2)}, u32[]{:S(2)}) collective-permute-start(bf16[128,896]{1,0:T(8,128)(2,1)S(1)} %collective-permute-done.11), channel_id=1, source_target_pairs={{0,480},{32,0},{64,32},{96,64},{128,96},{160,128},{192,160},{224,1... | collective-permute-start | bytes 688136 | tf_op jit(solution)/shard_map/ppermute | solution.py:18
  301.9 10.2 %collective-permute-start.6 = (bf16[128,896]{1,0:T(8,128)(2,1)S(1)}, bf16[128,896]{1,0:T(8,128)(2,1)}, u32[]{:S(2)}, u32[]{:S(2)}) collective-permute-start(bf16[128,896]{1,0:T(8,128)(2,1)S(1)} %collective-permute-done.5), channel_id=1, source_target_pairs={{0,32},{32,64},{64,96},{96,128},{128,160},{160,192},{192,224},{224... | collective-permute-start | bytes 688136 | tf_op jit(solution)/shard_map/ppermute | solution.py:16
  304.1 11.5 %collective-permute-start.13 = (bf16[128,896]{1,0:T(8,128)(2,1)S(1)}, bf16[128,896]{1,0:T(8,128)(2,1)S(1)}, u32[]{:S(2)}, u32[]{:S(2)}) collective-permute-start(bf16[128,896]{1,0:T(8,128)(2,1)S(1)} %collective-permute-done.12), channel_id=1, source_target_pairs={{0,480},{32,0},{64,32},{96,64},{128,96},{160,128},{192,160},{224,1... | collective-permute-start | bytes 688136 | tf_op jit(solution)/shard_map/ppermute | solution.py:18
  312.1 10.4 %collective-permute-start.7 = (bf16[128,896]{1,0:T(8,128)(2,1)}, bf16[128,896]{1,0:T(8,128)(2,1)}, u32[]{:S(2)}, u32[]{:S(2)}) collective-permute-start(bf16[128,896]{1,0:T(8,128)(2,1)} %collective-permute-done.6), channel_id=1, source_target_pairs={{0,32},{32,64},{64,96},{96,128},{128,160},{160,192},{192,224},{224... | collective-permute-start | bytes 688136 | tf_op jit(solution)/shard_map/ppermute | solution.py:16
  315.7 190.8 %collective-permute-start.14 = (bf16[128,896]{1,0:T(8,128)(2,1)S(1)}, bf16[128,896]{1,0:T(8,128)(2,1)}, u32[]{:S(2)}, u32[]{:S(2)}) collective-permute-start(bf16[128,896]{1,0:T(8,128)(2,1)S(1)} %collective-permute-done.13), channel_id=1, source_target_pairs={{0,480},{32,0},{64,32},{96,64},{128,96},{160,128},{192,160},{224,1... | collective-permute-start | bytes 688136 | tf_op jit(solution)/shard_map/ppermute | solution.py:18
  498.5 141.9 %all-gather.8.cloned.1.call-start = ((), (), s32[]{:S(2)}) async-start(), calls=%async_computation.6 | async-start | bytes 1081344 | tf_op jit(solution)/shard_map/all_gather | solution.py:154
  523.8 214.6 %copy-start.7 = (s32[16]{0:T(128)S(1)}, s32[16]{0:T(128)}, u32[]{:S(2)}) copy-start(s32[16]{0:T(128)} %param.28) | copy-start | bytes 196
Sparse Core Ops, SparseCore 0:
  92.1 65.2 all-gather.9
  159.6 67.8 all-gather.5
  230.2 105.9 reduce-scatter.4
  339.1 107.5 reduce-scatter.2
Sparse Core Ops, SparseCore 1:
  234.5 71.9 all-gather.13
  498.6 71.7 all-gather.11
  572.3 68.0 all-gather.7
